TPU v7x, 32 devices: a whole 2x2x4 slice. The times are simulated.
32 devices in a mesh: clus: 16 (over z, y, x), sub: 2 (over core).
Axes of the slice: x: 2, y: 2, z: 4, core: 2. Of those that a mesh axis runs over, the one named last changes fastest.
Arguments:
- dual_ops: float32 [64, 1536, 1536], P(('clus', 'sub')), may hold values from 0 to 3, as said below
- rigid_modes: float32 [64, 6, 1536], P(('clus', 'sub')), may hold values from -6 to 6
- members: int32 [64, 4, 1536], P(('clus', 'sub')), may hold values from 0 to 6144, as said below
- coarse_inverse: float32 [384, 384], P(('clus', 'sub')), may hold values from -1 to 1
- dual_rhs: float32 [64, 1536, 128], P(('clus', 'sub')), may hold values from -12 to 12
- coarse_rhs: float32 [64, 6, 128], P(('clus', 'sub')), may hold values from -512 to 512
Outputs:
- multipliers: float32 [64, 1536, 128], P(('clus', 'sub'))
- projected: float32 [64, 1536, 128], P(('clus', 'sub'))
Inputs may be any that keep to these rules, and one draw needn't show every extreme that they name: Every slot's group lists the slot itself first (its own position (s % 2) * 1536 + i), holds 1 to 4 slots of different subdomains, and is the same set for every slot in it; the group of every slot i >= 256 is that slot and one slot >= 256 of the other subdomain of the same device (members[s, 2:, i] = EMPTY); exported entries name only slots among the first 256 of a subdomain on devices with o in 0, 1, 2 that exist. Number the exported slots of a device k = 256 j + i for slot i of its j-th subdomain, and let E = 512: those with k < E / 4 are named only by groups of the other device of the same cluster; E / 4 <= k < E / 2 only by the device of cluster c + 1 with the same t; E / 2 <= k < 3 E / 4 only by the device of cluster c - 1 with the same t; 3 E / 4 <= k < 7 E / 8 only by the other device of the same cluster and the devices of cluster c + 1; 7 E / 8 <= k only by the other device of the same cluster and the devices of cluster c - 1. In each dual_ops[s] every row's off-diagonal entries sum in magnitude to less than its diagonal entry.
All inputs are finite; a program needn't handle non-finite values.
Results may differ from a plain program's by a relative error of at most 0.00015.
Values sent between devices are 32-bit elements; how exact they have to be, the bound alone decides.
A program may use at most 128 MiB of HBM per device.

v0:
```python
import jax
import jax.numpy as jnp
from jax import lax
from jax.sharding import PartitionSpec as P

ESUB = 256
ITERS = 2


def shifted(value, axis, steps):
    count = lax.axis_size(axis)
    leading, last = (max(0, -steps), min(count, count - steps))
    return lax.ppermute(value, axis, [(source, source + steps) for source in range(leading, last)])


def pair_product(first_field, second_field):
    return jnp.sum(first_field * second_field, axis=(0, 1))


def square_sum(field):
    return lax.psum(pair_product(field, field), ("clus", "sub"))


def on_device(dual_ops, rigid_modes, members, coarse_inverse, dual_rhs, coarse_rhs):
    sub_count, slot_count, load_cases = dual_rhs.shape
    local_rows = sub_count * slot_count
    export_rows = sub_count * ESUB
    pad_index = local_rows + 6 * export_rows
    quarter = export_rows // 4
    eighth = export_rows // 8
    share_rows = quarter + 4 * eighth
    group_count = members.shape[1]
    tables = jnp.transpose(members, (1, 0, 2)).reshape(group_count, local_rows)
    group_size = jnp.sum((tables < pad_index).astype(jnp.float32), axis=0)[:, None]
    offset = tables - local_rows
    cycle_block = offset // export_rows
    within = offset % export_rows
    inside = (tables >= local_rows) & (tables < pad_index)
    own_half = lax.axis_index("sub")
    neighbour = cycle_block // 2
    source_half = cycle_block % 2
    from_own = source_half == own_half
    above_start = local_rows + quarter + eighth
    pair_start = above_start + quarter + eighth
    shared_base = pair_start + source_half * share_rows
    lower_rows = jnp.where(
        within < 2 * quarter,
        local_rows + within - quarter,
        jnp.where(
            from_own,
            local_rows + quarter + within - 3 * quarter,
            shared_base + quarter + 2 * eighth + within - 3 * quarter,
        ),
    )
    upper_rows = jnp.where(
        within < 3 * quarter,
        above_start + within - 2 * quarter,
        jnp.where(
            from_own,
            above_start + quarter + within - 3 * quarter - eighth,
            shared_base + quarter + 3 * eighth + within - 3 * quarter - eighth,
        ),
    )
    pair_rows = jnp.where(
        within < quarter, shared_base + within, shared_base + quarter + within - 3 * quarter
    )
    remote = jnp.where(neighbour == 0, lower_rows, jnp.where(neighbour == 1, pair_rows, upper_rows))
    empty_at = pair_start + 2 * share_rows
    tables = jnp.where(tables < local_rows, tables, jnp.where(inside, remote, empty_at))
    other_members = tables[1:].reshape(-1)
    empty_row = jnp.zeros((1, load_cases), jnp.float32)

    def jump_part(field):
        flat_field = field.reshape(local_rows, load_cases)
        outgoing = field[:, :ESUB, :].reshape(export_rows, load_cases)
        upward = jnp.concatenate(
            [outgoing[quarter : 2 * quarter], outgoing[3 * quarter : 3 * quarter + eighth]], axis=0
        )
        downward = jnp.concatenate(
            [outgoing[2 * quarter : 3 * quarter], outgoing[3 * quarter + eighth :]], axis=0
        )
        below = shifted(upward, "clus", 1)
        above = shifted(downward, "clus", -1)
        shared = jnp.concatenate(
            [outgoing[:quarter], outgoing[3 * quarter :], below[quarter:], above[quarter:]], axis=0
        )
        gathered = jnp.concatenate(
            [below, above, lax.all_gather(shared, "sub", axis=0, tiled=True)], axis=0
        )
        pool_rows = jnp.concatenate([flat_field, gathered, empty_row], axis=0)
        picked = jnp.take(pool_rows, other_members, axis=0).reshape(
            group_count - 1, local_rows, load_cases
        )
        group_total = flat_field
        for member in range(group_count - 1):
            group_total = group_total + picked[member]
        return (flat_field - group_total / group_size).reshape(field.shape)

    def lift(terms):
        weights = jnp.dot(
            coarse_inverse,
            lax.all_gather(terms, ("clus", "sub"), axis=0, tiled=True),
            precision=lax.Precision.HIGHEST,
            preferred_element_type=jnp.float32,
        )
        weights = weights.reshape(sub_count, rigid_modes.shape[1], load_cases)
        return jump_part(
            jnp.einsum("jkm,jkn->jmn", rigid_modes, weights, precision=lax.Precision.HIGHEST)
        )

    def restrict(field):
        return jnp.einsum(
            "jkm,jmn->jkn", rigid_modes, field, precision=lax.Precision.HIGHEST
        ).reshape(-1, load_cases)

    def project(field):
        return field - lift(restrict(field))

    def blockwise(field):
        return jnp.einsum("jmq,jqn->jmn", dual_ops, field, precision=lax.Precision.HIGHEST)

    multipliers = lift(coarse_rhs.reshape(-1, load_cases))
    residual_now = jump_part(dual_rhs - blockwise(multipliers))
    projected = project(residual_now)
    direction = projected
    norm_now = square_sum(projected)
    for iteration in range(ITERS):
        along = jump_part(blockwise(direction))
        curvature_now = lax.psum(pair_product(direction, along), ("clus", "sub"))
        step_size = (norm_now / curvature_now)[None, None, :]
        multipliers = multipliers + step_size * direction
        residual_now = residual_now - step_size * along
        projected = project(residual_now)
        if iteration + 1 < ITERS:
            norm_next = square_sum(projected)
            direction = projected + (norm_next / norm_now)[None, None, :] * direction
            norm_now = norm_next
    return (multipliers, projected)


def solution(mesh):
    return jax.shard_map(
        on_device,
        mesh=mesh,
        in_specs=(
            P(("clus", "sub"), None, None),
            P(("clus", "sub"), None, None),
            P(("clus", "sub"), None, None),
            P(("clus", "sub"), None),
            P(("clus", "sub"), None, None),
            P(("clus", "sub"), None, None),
        ),
        out_specs=(P(("clus", "sub"), None, None), P(("clus", "sub"), None, None)),
        check_vma=False,
    )
```

profile of v0, /device:TPU:0, one launch (start us, length us, event | category | flops | bytes accessed | tf_op | source)
XLA Modules:
  0.0 818.7 jit_solution(16906384568805584855)
XLA Ops:
  1.4 43.9 %all-gather = f32[32,12,128]{2,1,0:T(8,128)S(1)} all-gather(f32[1,12,128]{2,1,0:T(8,128)S(1)} %reshape.286), channel_id=1, replica_groups=mesh['clus'=16,'sub'=2] {'clus','sub'}, dimensions={0}, use_global_device_ids=true | all-gather | bytes 202752 | tf_op jit(solution)/shard_map/all_gather | solution.py:102
  54.3 3.0 copy.77
  57.5 2.1 all_gather.34
  60.2 30.9 %gather_fusion = f32[9216,128]{1,0:T(8,128)} fusion(f32[4225,128]{1,0:T(8,128)S(1)} %dynamic-update-slice.34, s32[9216]{0:T(1024)S(1)} %fusion.17), kind=kCustom, calls=%fused_computation.clone | custom fusion | bytes 9474048 | tf_op jit(solution)/shard_map/jit(_take)/gather | solution.py:91
  91.1 6.6 broadcast_select_fusion.6
  99.2 3.1 copy.74
  105.6 3.2 divide_subtract_fusion.3
  108.8 23.3 %fusion = f32[2,1536,128]{1,2,0:T(8,128)S(1)} fusion(f32[2,1536,128]{1,2,0:T(8,128)S(1)} %copy-done.24, f32[2,1536,128]{1,2,0:T(8,128)S(1)} %divide_subtract_fusion.3, f32[2,1536,1536]{2,1,0:T(8,128)} %param.8), kind=kOutput, calls=%fused_computation.14 | convolution fusion | flops 7248150528 | bytes 23592960 | tf_op jit(solution)/shard_map/jmq,jqn->jmn/dot_general | solution.py:120
  133.9 4.6 collective-permute-start.2
  141.3 3.7 collective-permute-done.3
  145.0 2.1 all_gather.35
  147.3 30.9 %gather_fusion.1 = f32[9216,128]{1,0:T(8,128)} fusion(f32[4225,128]{1,0:T(8,128)S(1)} %dynamic-update-slice.29, s32[9216]{0:T(1024)S(1)} %fusion.17), kind=kCustom, calls=%fused_computation.1.clone | custom fusion | bytes 9474048 | tf_op jit(solution)/shard_map/jit(_take)/gather | solution.py:91
  178.3 6.6 broadcast_select_fusion.5
  186.4 3.0 copy.80
  192.7 3.0 divide_subtract_fusion.2
  198.3 38.8 %all-gather.1 = f32[32,12,128]{2,1,0:T(8,128)S(1)} all-gather(f32[1,12,128]{2,1,0:T(8,128)S(1)} %reshape.288), channel_id=1, replica_groups=mesh['clus'=16,'sub'=2] {'clus','sub'}, dimensions={0}, use_global_device_ids=true | all-gather | bytes 202752 | tf_op jit(solution)/shard_map/all_gather | solution.py:102
  240.7 2.2 collective-permute-start.4
  245.7 1.8 collective-permute-done.4
  247.6 2.0 collective-permute-done.5
  249.6 2.1 all_gather.37
  252.0 30.9 %gather_fusion.2 = f32[9216,128]{1,0:T(8,128)} fusion(f32[4225,128]{1,0:T(8,128)S(1)} %dynamic-update-slice.24, s32[9216]{0:T(1024)S(1)} %fusion.17), kind=kCustom, calls=%fused_computation.2.clone | custom fusion | bytes 9474048 | tf_op jit(solution)/shard_map/jit(_take)/gather | solution.py:91
  282.9 6.6 broadcast_select_fusion.4
  294.4 3.2 copy.89
  297.5 3.3 subtract_subtract_fusion.2
  300.8 23.3 %convolution_bitcast_fusion.3 = f32[2,1536,128]{1,2,0:T(8,128)S(1)} fusion(f32[2,1536,128]{1,2,0:T(8,128)S(1)} %subtract_subtract_fusion.2, f32[2,1536,1536]{2,1,0:T(8,128)} %param.8), kind=kOutput, calls=%fused_computation.10 | convolution fusion | flops 7247757312 | bytes 22020096 | tf_op jit(solution)/shard_map/jmq,jqn->jmn/dot_general | solution.py:120
  326.0 3.1 collective-permute-start.6
  333.6 2.1 collective-permute-done.7
  335.7 2.1 all_gather.38
  338.3 30.9 %gather_fusion.3 = f32[9216,128]{1,0:T(8,128)} fusion(f32[4225,128]{1,0:T(8,128)S(1)} %dynamic-update-slice.19, s32[9216]{0:T(1024)S(1)} %fusion.17), kind=kCustom, calls=%fused_computation.3.clone | custom fusion | bytes 9474048 | tf_op jit(solution)/shard_map/jit(_take)/gather | solution.py:91
  369.2 6.6 broadcast_select_fusion.3
  377.3 3.1 copy.93
  383.7 4.7 multiply_reduce_fusion.2
  388.4 37.2 %all-reduce = (f32[128]{0:T(128)S(1)}, f32[128]{0:T(128)S(1)}) all-reduce(f32[128]{0:T(128)S(1)} %get-tuple-element.10, f32[128]{0:T(128)S(1)} %get-tuple-element.9), channel_id=1, replica_groups=mesh['clus'=16,'sub'=2] {'clus','sub'}, use_global_device_ids=true, to_apply=%region_2.4 | all-reduce | flops 256 | bytes 2048 | tf_op jit(solution)/shard_map/psum | solution.py:21
  425.6 1.8 multiply_subtract_fusion.1
  429.9 41.2 %all-gather.2 = f32[32,12,128]{2,1,0:T(8,128)S(1)} all-gather(f32[1,12,128]{2,1,0:T(8,128)S(1)} %reshape.290), channel_id=1, replica_groups=mesh['clus'=16,'sub'=2] {'clus','sub'}, dimensions={0}, use_global_device_ids=true | all-gather | bytes 202752 | tf_op jit(solution)/shard_map/all_gather | solution.py:102
  478.8 2.1 collective-permute-done.8
  480.9 2.0 collective-permute-done.9
  483.0 2.1 all_gather.40
  485.2 30.9 %gather_fusion.4 = f32[9216,128]{1,0:T(8,128)} fusion(f32[4225,128]{1,0:T(8,128)S(1)} %dynamic-update-slice.14, s32[9216]{0:T(1024)S(1)} %fusion.17), kind=kCustom, calls=%fused_computation.4.clone | custom fusion | bytes 9474048 | tf_op jit(solution)/shard_map/jit(_take)/gather | solution.py:91
  516.1 6.6 broadcast_select_fusion.2
  524.2 3.1 copy.101
  530.6 4.8 multiply_reduce_fusion.1
  535.4 37.0 %psum.30 = f32[128]{0:T(128)S(1)} all-reduce(f32[128]{0:T(128)S(1)} %get-tuple-element.15), channel_id=1, replica_groups=mesh['clus'=16,'sub'=2] {'clus','sub'}, use_global_device_ids=true, to_apply=%region_6.8 | all-reduce | flops 128 | bytes 1024 | tf_op jit(solution)/shard_map/psum | solution.py:21
  572.4 22.5 %convolution_bitcast_fusion.1 = f32[2,1536,128]{1,2,0:T(8,128)S(1)} fusion(f32[2,1536,1536]{2,1,0:T(8,128)} %param.8, f32[2,1536,128]{1,2,0:T(8,128)} %get-tuple-element.16, f32[2,1536,128]{1,2,0:T(8,128)S(1)} %copy-done.3, f32[128]{0:T(128)S(1)} %div.94), kind=kOutput, calls=%fused_computation.8 | convolution fusion | flops 7248543744 | bytes 23593472 | tf_op jit(solution)/shard_map/jmq,jqn->jmn/dot_general | solution.py:120
  595.1 1.7 copy.104
  596.8 4.2 collective-permute-start.10
  603.8 3.7 collective-permute-done.11
  607.5 2.1 all_gather.41
  609.7 30.9 %gather_fusion.5 = f32[9216,128]{1,0:T(8,128)} fusion(f32[4225,128]{1,0:T(8,128)S(1)} %dynamic-update-slice.9, s32[9216]{0:T(1024)S(1)} %fusion.17), kind=kCustom, calls=%fused_computation.5.clone | custom fusion | bytes 9474048 | tf_op jit(solution)/shard_map/jit(_take)/gather | solution.py:91
  640.7 6.6 broadcast_select_fusion.1
  648.8 3.1 copy.106
  651.9 1.7 copy.108
  655.2 5.3 multiply_reduce_fusion
  660.5 41.6 %psum.31 = f32[128]{0:T(128)S(1)} all-reduce(f32[128]{0:T(128)S(1)} %get-tuple-element.13), channel_id=1, replica_groups=mesh['clus'=16,'sub'=2] {'clus','sub'}, use_global_device_ids=true, to_apply=%region_8.10 | all-reduce | flops 128 | bytes 1024 | tf_op jit(solution)/shard_map/psum | solution.py:129
  702.2 3.1 convolution_bitcast_fusion.8
  705.2 41.2 %all-gather.3 = f32[32,12,128]{2,1,0:T(8,128)S(1)} all-gather(f32[1,12,128]{2,1,0:T(8,128)S(1)} %reshape.292), channel_id=1, replica_groups=mesh['clus'=16,'sub'=2] {'clus','sub'}, dimensions={0}, use_global_device_ids=true | all-gather | bytes 202752 | tf_op jit(solution)/shard_map/all_gather | solution.py:102
  754.2 2.1 collective-permute-done.12
  756.3 2.0 collective-permute-done.13
  758.3 2.1 all_gather.43
  760.5 30.9 %gather_fusion.6 = f32[9216,128]{1,0:T(8,128)} fusion(f32[4225,128]{1,0:T(8,128)S(1)} %dynamic-update-slice.4, s32[9216]{0:T(1024)S(1)} %fusion.17), kind=kCustom, calls=%fused_computation.6.clone | custom fusion | bytes 9474048 | tf_op jit(solution)/shard_map/jit(_take)/gather | solution.py:91
  791.5 6.6 broadcast_select_fusion
  802.9 3.2 copy.115
  806.1 7.6 subtract_subtract_fusion
  813.7 3.1 copy.118
  (232 shorter events, 85.6 us)
Async XLA Ops:
  0.6 45.7 %copy-start = (f32[2,6,1536]{2,0,1:T(2,128)S(1)}, f32[2,6,1536]{2,0,1:T(2,128)}, u32[]{:S(2)}) copy-start(f32[2,6,1536]{2,0,1:T(2,128)} %param.9) | copy-start | bytes 221188
  46.3 4.3 copy-start.26
  47.8 3.4 copy-start.19
  48.0 9.4 %collective-permute-start = (f32[192,128]{1,0:T(8,128)S(1)}, f32[192,128]{1,0:T(8,128)S(1)}, u32[]{:S(2)}, u32[]{:S(2)}) collective-permute-start(f32[192,128]{1,0:T(8,128)S(1)} %pad_maximum_fusion.7), channel_id=1, source_target_pairs={{0,2},{2,4},{4,6},{6,8},{8,10},{10,12},{12,14},{14,16},{16,18},{18... | collective-permute-start | bytes 294920 | tf_op jit(solution)/shard_map/ppermute | solution.py:13
  49.3 8.1 collective-permute-start.1
  103.9 1.6 copy-start.20
  105.6 3.2 copy-start.24
  108.7 23.3 %copy-start.23 = (f32[2,1536,128]{1,2,0:T(8,128)}, f32[2,1536,128]{1,2,0:T(8,128)S(1)}, u32[]{:S(2)}) copy-start(f32[2,1536,128]{1,2,0:T(8,128)S(1)} %divide_subtract_fusion.3) | copy-start | bytes 4718596
  132.0 1.8 copy-start.17
  133.9 7.4 collective-permute-start.2
  138.4 6.5 collective-permute-start.3
  191.0 1.7 copy-start.18
  195.7 1.1 copy-start.10
  196.9 40.2 %copy-start.27 = (f32[12,384]{1,0:T(8,128)S(1)}, f32[12,384]{1,0:T(8,128)}, u32[]{:S(2)}) copy-start(f32[12,384]{1,0:T(8,128)} %param.11) | copy-start | bytes 55300
  238.8 1.9 copy-start.15
  240.7 6.8 collective-permute-start.4
  242.9 6.7 collective-permute-start.5
  294.4 3.2 copy-start.11
  294.4 3.2 copy-start.16
  300.8 23.3 %copy-start.1 = (f32[2,1536,128]{1,2,0:T(8,128)}, f32[2,1536,128]{1,2,0:T(8,128)S(1)}, u32[]{:S(2)}) copy-start(f32[2,1536,128]{1,2,0:T(8,128)S(1)} %subtract_subtract_fusion.2) | copy-start | bytes 4718596
  324.2 1.9 copy-start.22
  326.0 7.5 collective-permute-start.6
  329.2 6.5 collective-permute-start.7
  382.0 1.6 copy-start.2
  383.7 41.9 %copy-start.12 = (f32[2,1536,128]{1,2,0:T(8,128)S(1)}, f32[2,1536,128]{1,2,0:T(8,128)}, u32[]{:S(2)}) copy-start(f32[2,1536,128]{1,2,0:T(8,128)} %copy-done.10) | copy-start | bytes 4718596
  427.3 1.1 copy-start.6
  472.8 1.9 copy-start.13
  474.7 6.2 collective-permute-start.8
  476.0 6.9 collective-permute-start.9
  528.9 1.6 copy-start.7
  530.6 41.9 %copy-start.3 = (f32[2,1536,128]{1,2,0:T(8,128)S(1)}, f32[2,1536,128]{1,2,0:T(8,128)}, u32[]{:S(2)}) copy-start(f32[2,1536,128]{1,2,0:T(8,128)} %copy-done.1) | copy-start | bytes 4718596
  594.9 1.9 copy-start.14
  596.8 7.0 collective-permute-start.10
  601.0 6.5 collective-permute-start.11
  653.6 1.6 copy-start.4
  655.2 46.9 %copy-start.8 = (f32[2,1536,128]{1,2,0:T(8,128)S(1)}, f32[2,1536,128]{1,2,0:T(8,128)}, u32[]{:S(2)}) copy-start(f32[2,1536,128]{1,2,0:T(8,128)} %copy-done.6) | copy-start | bytes 4718596
  748.1 1.9 copy-start.21
  750.0 6.2 collective-permute-start.12
  751.4 6.9 collective-permute-start.13
  802.9 3.2 copy-start.5
  802.9 3.2 copy-start.9
  813.7 3.1 copy-start.25
where the time goes:
time: 824 us; the launch traced here: 819 us
  local copies, waits for them, and re-layouts  308 us (37%)
  blocking collectives  295 us (36%)
  matrix products  82.4 us (10%)
  other arithmetic  80.8 us (10%)
  starting transfers between devices  26.9 us (3%)
  waiting for transfers between devices  23.1 us (3%)
    gather x7, local copies, waits for them, and re-layouts, jump_part(): jnp.take(pool_rows, other_members, axis=0)  217 us
    all_gather x4, blocking collectives, lift(): lax.all_gather(terms, ('clus', 'sub'), axis=0, tiled=True)  165 us
    psum x2, blocking collectives, square_sum(): return lax.psum(pair_product(field, field), ('clus', 'sub'))  74.2 us
    dot_general x3, matrix products, blockwise(): jnp.einsum('jmq,jqn->jmn', dual_ops, field, precision=lax.Precision.HIGHEST)  69.1 us
    select_n x7, other arithmetic, jump_part(): jnp.take(pool_rows, other_members, axis=0)  46.4 us
    squeeze x21, local copies, waits for them, and re-layouts, jump_part(): group_total = group_total + picked[member]  44.6 us
    psum x1, blocking collectives, on_device(): curvature_now = lax.psum(pair_product(direction, along), ('clus', 'sub'))  41.6 us
    ppermute x14, starting transfers between devices, shifted(): lax.ppermute(value, axis, [(source, source + steps) for source in range(l...  26.9 us
  transfers between devices with their start and end apart: 14, of which 10 were waited for; matrix products, arithmetic and copies ran while one was open for 2% of the time, Pallas kernels for 0%

commit v1 on v0

v1 whole, which is shorter than its diff:
```python
import functools
import jax
import jax.numpy as jnp
from jax import lax
from jax.experimental import pallas as pl
from jax.experimental.pallas import tpu as pltpu
from jax.sharding import PartitionSpec as P

ESUB = 256
LANES = 128
TILE = 256
BIG = 512
POOL = 768
ROUNDS = 4
MESH = pl.DeviceIdType.MESH
F32 = jnp.float32
BF16 = jnp.bfloat16


def split(value):
    high = value.astype(BF16)
    low = (value - high.astype(F32)).astype(BF16)
    return jnp.concatenate([high, low], axis=1)


def mm(left, right):
    return jnp.dot(left, right, preferred_element_type=F32)


def fold(wide):
    return wide[:, :LANES] + wide[:, LANES:]


def kernel(
    ops_hbm, modes_field, modes, inner0, inner1, outer, cinv, rhs, crhs,
    mult, proj,
    ops_hi, ops_lo, ops_buf, perm0, perm1, share, lift_cat, image_cat, cat,
    field, jumped, image, past, pool, coarse, near,
    ops_sem, halo_send, halo_recv, near_send, near_recv, ag_send, ag_recv, fwd_send, fwd_recv,
    *, clusters,
):
    c = lax.axis_index("clus")
    t = lax.axis_index("sub")
    other = 1 - t
    has_up = c < clusters - 1
    has_down = c > 0
    up = jnp.minimum(c + 1, clusters - 1)
    down = jnp.maximum(c - 1, 0)
    slot = (c % 4) * 2 + t
    half = ops_hi.shape[0] // 2
    tiles = 2 * ops_hi.shape[0]
    per = tiles // 2
    rows = per * TILE
    inner = rows - ESUB

    def load(chunk, buf):
        return pltpu.make_async_copy(ops_hbm.at[chunk], ops_buf.at[buf], ops_sem.at[buf])

    load(0, 0).start()
    load(1, 1).start()

    near[...] = jnp.zeros_like(near)
    barrier = pltpu.get_barrier_semaphore()

    @pl.loop(1, clusters)
    def _(k):
        pl.semaphore_signal(barrier, inc=1, device_id=((c + k) % clusters, t), device_id_type=MESH)

    pl.semaphore_signal(barrier, inc=1, device_id=(c, other), device_id_type=MESH)

    @pl.when(has_up)
    def _():
        pl.semaphore_signal(barrier, inc=1, device_id=(up, other), device_id_type=MESH)

    @pl.when(has_down)
    def _():
        pl.semaphore_signal(barrier, inc=1, device_id=(down, other), device_id_type=MESH)

    @pl.when(c == 0)
    def _():
        for r in range(ROUNDS):
            pool[r, 256:448, :] = jnp.zeros((192, LANES), F32)
            pool[r, 640:704, :] = jnp.zeros((64, LANES), F32)

    @pl.when(c == clusters - 1)
    def _():
        for r in range(ROUNDS):
            pool[r, 448:640, :] = jnp.zeros((192, LANES), F32)
            pool[r, 704:768, :] = jnp.zeros((64, LANES), F32)

    coarse[0, t, c] = crhs[...]
    near[slot] = cinv[...]

    @pl.when(has_up & has_down)
    def _():
        pl.semaphore_wait(barrier, clusters + 2)

    @pl.when(jnp.logical_not(has_up & has_down))
    def _():
        pl.semaphore_wait(barrier, clusters + 1)

    def halo_copies(source, r):
        top, low = source.at[0], source.at[per]
        plan = [
            (top, 0, 128, 0, (c, other)),
            (low, 128, 128, 128, (c, other)),
            (top, 128, 128, 256, (up, t)),
            (low, 128, 64, 384, (up, t)),
            (low, 128, 64, 640, (up, other)),
            (low, 0, 128, 448, (down, t)),
            (low, 192, 64, 576, (down, t)),
            (low, 192, 64, 704, (down, other)),
        ]
        copies = [
            pltpu.make_async_remote_copy(
                src_ref=ref.at[pl.ds(start, size)],
                dst_ref=pool.at[r, pl.ds(to, size)],
                send_sem=halo_send.at[r, n],
                recv_sem=halo_recv.at[r, n],
                device_id=device,
                device_id_type=MESH,
            )
            for n, (ref, start, size, to, device) in enumerate(plan)
        ]
        return copies[:2], copies[2:5], copies[5:]

    def near_copies():
        return [
            pltpu.make_async_remote_copy(
                src_ref=cinv,
                dst_ref=near.at[slot],
                send_sem=near_send.at[n],
                recv_sem=near_recv.at[n],
                device_id=device,
                device_id_type=MESH,
            )
            for n, device in enumerate([(c, other), (up, t), (up, other), (down, t), (down, other)])
        ]

    def start_all(groups):
        both, ups, downs = groups

        @pl.when(has_up)
        def _():
            for copy in ups:
                copy.start()

        @pl.when(has_down)
        def _():
            for copy in downs:
                copy.start()

        for copy in both:
            copy.start()

    def wait_all(groups):
        both, ups, downs = groups
        for copy in both:
            copy.wait_recv()
            copy.wait_send()

        @pl.when(has_up)
        def _():
            for copy in ups:
                copy.wait_send()
            for copy in downs:
                copy.wait_recv()

        @pl.when(has_down)
        def _():
            for copy in downs:
                copy.wait_send()
            for copy in ups:
                copy.wait_recv()

    def near_groups():
        copies = near_copies()
        return copies[:1], copies[1:3], copies[3:]

    def ag_copy(r, k):
        return pltpu.make_async_remote_copy(
            src_ref=coarse.at[r, t, c],
            dst_ref=coarse.at[r, t, c],
            send_sem=ag_send.at[r, k],
            recv_sem=ag_recv.at[r, k],
            device_id=((c + k) % clusters, t),
            device_id_type=MESH,
        )

    def ag_arrival(r, k):
        source = (c + clusters - k) % clusters
        return pltpu.make_async_remote_copy(
            src_ref=coarse.at[r, t, source],
            dst_ref=coarse.at[r, t, source],
            send_sem=ag_send.at[r, k],
            recv_sem=ag_recv.at[r, k],
            device_id=((c + k) % clusters, t),
            device_id_type=MESH,
        )

    def ag_start(r):
        @pl.loop(1, clusters)
        def _(k):
            ag_copy(r, k).start()

    def fwd_copy(r, which):
        return pltpu.make_async_remote_copy(
            src_ref=coarse.at[r, which],
            dst_ref=coarse.at[r, which],
            send_sem=fwd_send.at[r],
            recv_sem=fwd_recv.at[r],
            device_id=(c, other),
            device_id_type=MESH,
        )

    def ag_forward(r):
        @pl.loop(1, clusters)
        def _(k):
            ag_arrival(r, k).wait_recv()

        fwd_copy(r, t).start()

    def ag_finish(r):
        @pl.loop(1, clusters)
        def _(k):
            ag_copy(r, k).wait_send()

        fwd_copy(r, t).wait_send()
        fwd_copy(r, other).wait_recv()
        gathered = coarse[r].reshape(2 * clusters * 16, LANES)
        weights = jnp.dot(
            near[...].reshape(LANES, 2 * clusters * 16), gathered,
            precision=lax.Precision.HIGHEST, preferred_element_type=F32,
        )
        high = weights.astype(BF16)
        low = (weights - high.astype(F32)).astype(BF16)
        wide = jnp.concatenate(
            [jnp.concatenate([high, low], axis=1), jnp.concatenate([high, jnp.zeros_like(high)], axis=1)],
            axis=0,
        )
        return wide, jnp.sum(gathered.reshape(2 * clusters, 16, LANES), axis=0)

    start_all(halo_copies(modes_field, 0))
    start_all(near_groups())
    ag_start(0)

    @pl.loop(0, inner // TILE)
    def _(n):
        at = lax.broadcasted_iota(jnp.int32, (TILE, inner), 0) + n * TILE
        perm0[n] = (at == inner1[...]).astype(F32).astype(BF16)
        perm1[n] = (at == inner0[...]).astype(F32).astype(BF16)

    columns = jnp.transpose(outer[...])
    at = lax.broadcasted_iota(jnp.int32, (2 * ESUB, POOL), 1).astype(F32)
    total = jnp.zeros((2 * ESUB, POOL), F32)
    for n in range(3):
        total = total + (at == columns[:, n : n + 1]).astype(F32)
    share[...] = total.astype(BF16)

    def portion():
        return jnp.transpose(outer[...])[:, 3:4]

    @pl.loop(0, 2 * half)
    def _(chunk):
        buf = chunk % 2
        load(chunk, buf).wait()

        @pl.loop(0, BIG // 64)
        def _(n):
            at_rows = pl.ds(pl.multiple_of(n * 64, 64), 64)
            value = ops_buf[buf, at_rows, :]
            high = value.astype(BF16)
            ops_hi[chunk, at_rows, :] = high
            ops_lo[chunk, at_rows, :] = (value - high.astype(F32)).astype(BF16)

        @pl.when(chunk + 2 < 2 * half)
        def _():
            load(chunk + 2, buf).start()

    def tile_rows(n):
        return pl.ds(pl.multiple_of(n * TILE, TILE), TILE)

    def make_cat(source):
        @pl.loop(0, tiles)
        def _(n):
            cat[tile_rows(n), :] = split(source[n])

    def jump(source, r, groups, target):
        @pl.loop(0, inner // TILE)
        def _(n):
            picked = fold(mm(perm0[n], cat[rows + ESUB : 2 * rows, :]))
            target[1 + n] = 0.5 * (source[1 + n] - picked)
            back = fold(mm(perm1[n], cat[ESUB:rows, :]))
            target[per + 1 + n] = 0.5 * (source[per + 1 + n] - back)

        wait_all(groups)
        picked = fold(mm(share[...], split(pool[r])))
        scale = portion()
        target[0] = source[0] - (source[0] + picked[:ESUB]) * scale[:ESUB]
        target[per] = source[per] - (source[per] + picked[ESUB:]) * scale[ESUB:]

    def big_tile(n, emit):
        at_rows = pl.ds(pl.multiple_of((n // half) * rows, TILE), rows)
        out = fold(mm(ops_hi[n], cat[at_rows, :])) + mm(ops_lo[n], cat[at_rows, :LANES])
        emit(n, out)

    def store_image(n, out):
        image[2 * n] = out[:TILE]
        image[2 * n + 1] = out[TILE:]

    def store_image_cat(n, out):
        image_cat[pl.ds(pl.multiple_of(n * BIG, BIG), BIG), :] = split(out)

    def restrict():
        value = modes[...]
        high = value.astype(BF16)
        low = (value - high.astype(F32)).astype(BF16)
        out = mm(jnp.concatenate([high, low], axis=0), cat[...])
        return fold(out[:16]) + out[16:, :LANES]

    def put(r, terms, sums):
        row = lax.broadcasted_iota(jnp.int32, (16, LANES), 0)
        for n, value in enumerate(sums):
            terms = jnp.where(row == 12 + n, value, terms)
        coarse[r, t, c] = terms

    def row_sum(value):
        return jnp.sum(value, axis=0, keepdims=True)

    make_cat(modes_field)
    jump(modes_field, 0, halo_copies(modes_field, 0), field)

    @pl.loop(0, tiles)
    def _(n):
        value = split(field[n])
        lift_cat[tile_rows(n), :] = value
        cat[tile_rows(n), :] = value

    ag_forward(0)

    @pl.loop(0, 2 * half)
    def _(n):
        big_tile(n, store_image_cat)

    wait_all(near_groups())
    wide, _ = ag_finish(0)

    def start_tile(n):
        mult[n] = fold(mm(lift_cat[tile_rows(n), :], wide))
        value = rhs[n] - fold(mm(image_cat[tile_rows(n), :], wide))
        field[n] = value
        cat[tile_rows(n), :] = split(value)

    start_tile(0)
    start_tile(per)
    groups = halo_copies(field, 1)
    start_all(groups)

    @pl.loop(1, per)
    def _(n):
        start_tile(n)
        start_tile(per + n)

    jump(field, 1, groups, jumped)
    make_cat(jumped)
    put(1, restrict(), [])
    ag_start(1)

    @pl.loop(0, half)
    def _(n):
        big_tile(n, store_image)

    ag_forward(1)

    @pl.loop(half, 2 * half)
    def _(n):
        big_tile(n, store_image)

    wide, _ = ag_finish(1)

    def first_tile(n, carry):
        value = jumped[n] - fold(mm(lift_cat[tile_rows(n), :], wide))
        proj[n] = value
        made = image[n] - fold(mm(image_cat[tile_rows(n), :], wide))
        field[n] = made
        cat[tile_rows(n), :] = split(made)
        return carry[0] + row_sum(value * made), carry[1] + row_sum(value * value)

    zero = jnp.zeros((1, LANES), F32)
    carry = first_tile(per, first_tile(0, (zero, zero)))
    groups = halo_copies(field, 2)
    start_all(groups)
    carry = lax.fori_loop(1, per, lambda n, now: first_tile(per + n, first_tile(n, now)), carry)
    jump(field, 2, groups, jumped)
    make_cat(jumped)
    put(2, restrict(), carry)
    ag_start(2)

    @pl.loop(0, half)
    def _(n):
        big_tile(n, store_image)

    ag_forward(2)

    @pl.loop(half, 2 * half)
    def _(n):
        big_tile(n, store_image)

    wide, sums = ag_finish(2)
    curvature, norm = sums[12:13], sums[13:14]
    step = norm / curvature

    def second_tile(n, carry):
        moved = jumped[n] - fold(mm(lift_cat[tile_rows(n), :], wide))
        past[n] = moved
        old = proj[n]
        mult[n] = mult[n] + step * old
        new = old - step * moved
        old_made = field[n]
        made = old_made - step * (image[n] - fold(mm(image_cat[tile_rows(n), :], wide)))
        image[n] = made
        proj[n] = new
        jumped[n] = old
        cat[tile_rows(n), :] = split(made)
        return (
            carry[0] + row_sum(new * made),
            carry[1] + row_sum(new * old_made + old * made),
            carry[2] + row_sum(new * new),
        )

    carry = second_tile(per, second_tile(0, (zero, zero, zero)))
    groups = halo_copies(image, 3)
    start_all(groups)
    carry = lax.fori_loop(1, per, lambda n, now: second_tile(per + n, second_tile(n, now)), carry)
    jump(image, 3, groups, field)
    make_cat(field)
    put(3, restrict(), carry)
    ag_start(3)
    ag_forward(3)
    wide, sums = ag_finish(3)
    fresh, crossed, norm_next = sums[12:13], sums[13:14], sums[14:15]
    beta = norm_next / norm
    step_last = norm_next / (fresh + beta * (crossed + beta * curvature))

    @pl.loop(0, tiles)
    def _(n):
        moved = field[n] - fold(mm(lift_cat[tile_rows(n), :], wide))
        old = proj[n]
        mult[n] = mult[n] + step_last * (old + beta * jumped[n])
        proj[n] = old - step_last * (moved + beta * past[n])


def on_device(clusters, dual_ops, rigid_modes, members, coarse_inverse, dual_rhs, coarse_rhs):
    subs, rows, lanes = dual_rhs.shape
    modes_count = rigid_modes.shape[1]
    tiles = subs * rows // TILE
    local_rows = subs * rows
    export = subs * ESUB
    pad_index = local_rows + 6 * export
    inner = rows - ESUB
    c = lax.axis_index("clus")
    t = lax.axis_index("sub")
    slot = (c % 4) * 2 + t

    inner0 = (members[0, 1, ESUB:] - rows - ESUB)[None, :]
    inner1 = (members[1, 1, ESUB:] - ESUB)[None, :]

    names = jnp.transpose(members[:, :, :ESUB], (1, 0, 2)).reshape(-1, export)
    offset = names - local_rows
    block = offset // export
    within = offset % export
    cluster = block // 2
    own = (block % 2) == t
    sibling = jnp.where(within < 128, within, within - 256)
    lower = jnp.where(own, jnp.where(within < 256, within + 128, within), within + 256)
    upper = jnp.where(own, jnp.where(within < 384, within + 192, within + 128), within + 256)
    at = jnp.where(cluster == 0, lower, jnp.where(cluster == 1, sibling, upper))
    at = jnp.where(names < pad_index, at, -1).astype(F32)
    size = jnp.sum((names < pad_index).astype(F32), axis=0, keepdims=True)
    outer = jnp.concatenate([at[1:4], 1.0 / size, jnp.zeros((4, export), F32)], axis=0)

    count = subs * modes_count
    modes = jnp.concatenate(
        [
            jnp.pad(rigid_modes[0], ((0, 16 - modes_count), (0, rows))),
        ],
        axis=0,
    ) + jnp.pad(rigid_modes[1], ((modes_count, 16 - count), (rows, 0)))
    lane = lax.broadcasted_iota(jnp.int32, (8, 1, 1), 0)
    spread = jnp.where(lane == slot, modes[None], 0.0).reshape(LANES, local_rows)
    modes_field = jnp.transpose(spread).reshape(tiles, TILE, lanes)

    cinv = coarse_inverse.reshape(count, clusters, 2, count).transpose(0, 2, 1, 3)
    cinv = jnp.pad(cinv, ((0, 16 - count), (0, 0), (0, 0), (0, 16 - count)))
    cinv = cinv.reshape(16, 2 * clusters * 16)
    crhs = jnp.pad(coarse_rhs.reshape(count, lanes), ((0, 16 - count), (0, 0)))

    big = local_rows // BIG
    vmem = pl.BlockSpec(memory_space=pltpu.VMEM)
    shape = jax.ShapeDtypeStruct((tiles, TILE, lanes), F32)
    mult, proj = pl.pallas_call(
        functools.partial(kernel, clusters=clusters),
        out_shape=(shape, shape),
        in_specs=[pl.BlockSpec(memory_space=pl.ANY)] + [vmem] * 8,
        out_specs=(vmem, vmem),
        scratch_shapes=[
            pltpu.VMEM((big, BIG, rows), BF16),
            pltpu.VMEM((big, BIG, rows), BF16),
            pltpu.VMEM((2, BIG, rows), F32),
            pltpu.VMEM((inner // TILE, TILE, inner), BF16),
            pltpu.VMEM((inner // TILE, TILE, inner), BF16),
            pltpu.VMEM((export, POOL), BF16),
            pltpu.VMEM((local_rows, 2 * lanes), BF16),
            pltpu.VMEM((local_rows, 2 * lanes), BF16),
            pltpu.VMEM((local_rows, 2 * lanes), BF16),
            pltpu.VMEM((tiles, TILE, lanes), F32),
            pltpu.VMEM((tiles, TILE, lanes), F32),
            pltpu.VMEM((tiles, TILE, lanes), F32),
            pltpu.VMEM((tiles, TILE, lanes), F32),
            pltpu.VMEM((ROUNDS, POOL, lanes), F32),
            pltpu.VMEM((ROUNDS, 2, clusters, 16, lanes), F32),
            pltpu.VMEM((8, 16, 2 * clusters * 16), F32),
            pltpu.SemaphoreType.DMA((2,)),
            pltpu.SemaphoreType.DMA((ROUNDS, 8)),
            pltpu.SemaphoreType.DMA((ROUNDS, 8)),
            pltpu.SemaphoreType.DMA((5,)),
            pltpu.SemaphoreType.DMA((5,)),
            pltpu.SemaphoreType.DMA((ROUNDS, clusters)),
            pltpu.SemaphoreType.DMA((ROUNDS, clusters)),
            pltpu.SemaphoreType.DMA((ROUNDS,)),
            pltpu.SemaphoreType.DMA((ROUNDS,)),
        ],
        compiler_params=pltpu.CompilerParams(
            collective_id=0, has_side_effects=True, vmem_limit_bytes=60 * 2**20
        ),
    )(
        dual_ops.reshape(big, BIG, rows), modes_field, modes, inner0, inner1, outer, cinv,
        dual_rhs.reshape(tiles, TILE, lanes), crhs,
    )
    return mult.reshape(subs, rows, lanes), proj.reshape(subs, rows, lanes)


def solution(mesh):
    spec = P(("clus", "sub"), None, None)
    return jax.shard_map(
        functools.partial(on_device, mesh.shape["clus"]),
        mesh=mesh,
        in_specs=(spec, spec, spec, P(("clus", "sub"), None), spec, spec),
        out_specs=(spec, spec),
        check_vma=False,
    )
```

time: 824 us -> 97.9 us (0.12)
  local copies, waits for them, and re-layouts: 308 us -> 10 us
  blocking collectives: 295 us -> 0 us
  Pallas kernels: 0 us -> 82.9 us
  matrix products: 82.4 us -> 0 us
  other arithmetic: 80.8 us -> 3.75 us
  starting transfers between devices: 26.9 us -> 0 us
  waiting for transfers between devices: 23.1 us -> 0 us
    gather x7 -> x0, local copies, waits for them, and re-layouts: 217 us -> none  [jump_part(): jnp.take(pool_rows, other_members, axis=0)]
    all_gather x11 -> x0, blocking collectives: 180 us -> none  [the longest x4 165 us: lift(): lax.all_gather(terms, ('clus', 'sub'), axis=0, tiled=True)]
    psum x3 -> x0, blocking collectives: 116 us -> none  [the longest x2 74.2 us: square_sum(): return lax.psum(pair_product(field, field), ('clus', 'sub'))]
    pallas_call x0 -> x1, Pallas kernels: none -> 82.9 us  [on_device(): pl.pallas_call(functools.partial(kernel, clusters=clusters), out_shape=(s...]
    dot_general x14 -> x0, matrix products: 82.4 us -> none  [the longest x3 69.1 us: blockwise(): jnp.einsum('jmq,jqn->jmn', dual_ops, field, precision=lax.Precision.HIGHEST)]
    select_n x8 -> x1, other arithmetic: 46.5 us -> 0.2 us  [on_device(): jnp.where(lane == slot, modes[None], 0.0).reshape(LANES, local_rows)]
    squeeze x21 -> x1, local copies, waits for them, and re-layouts: 44.6 us -> 0.01 us  [on_device(): rigid_modes[1]]
    ppermute x14 -> x0, starting transfers between devices: 26.9 us -> none  [shifted(): lax.ppermute(value, axis, [(source, source + steps) for source in range(l...]
  transfers between devices with their start and end apart: 14 -> 0, of which waited for: 10 -> 0; matrix products, arithmetic and copies ran while one was open for 2% -> 0% of each run, Pallas kernels for 0% -> 0%
where the time goes in v1:
time: 97.9 us; the launch traced here: 97.4 us
  Pallas kernels  82.9 us (85%)
  local copies, waits for them, and re-layouts  10 us (10%)
  other arithmetic  3.75 us (4%)
    pallas_call x1, Pallas kernels, on_device(): pl.pallas_call(functools.partial(kernel, clusters=clusters), out_shape=(s...  82.9 us
    unnamed x9, local copies, waits for them, and re-layouts  4.64 us

profile of v1, /device:TPU:0, one launch (start us, length us, event | category | flops | bytes accessed | tf_op | source)
XLA Modules:
  0.0 97.4 jit_solution(8121465560751083923)
XLA Ops:
  0.7 0.1 broadcast_in_dim.35
  0.7 0.1 broadcast_in_dim.36
  0.8 0.1 pad.22.clone
  0.9 0.7 convert_reduce_fusion
  1.6 0.7 copy.17
  2.3 0.6 pad.19.crhs
  3.0 0.7 slice_add_fusion
  3.7 1.4 %add_bitcast_fusion = (s32[1,1280]{1,0:T(1,128)}, s32[1,1280]{1,0:T(1,128)}) fusion(s32[2,4,1536]{2,1,0:T(4,128)} %param.8), kind=kLoop, calls=%fused_computation.32 | loop fusion | flops 2560 | bytes 20480 | tf_op jit(solution)/shard_map/sub | solution.py:466
  5.1 0.7 maximum_maximum_fusion.outer
  5.8 1.0 %fusion.8 = (f32[1,6,1536]{2,0,1:T(1,128)S(1)}, f32[1,6,1536]{2,0,1:T(1,128)S(1)}) fusion(f32[2,6,1536]{2,0,1:T(2,128)} %param.7), kind=kLoop, calls=%fused_computation.42 | loop fusion | bytes 147456 | tf_op jit(solution)/shard_map/slice | solution.py:485
  6.8 0.0 copy-start
  6.9 1.1 %reshape.83 = f32[12,16,2,12]{3,2,1,0:T(2,128)S(1)} reshape(f32[12,384]{1,0:T(8,128)} %param.9) | data formatting | bytes 36864 | tf_op jit(solution)/shard_map/reshape | solution.py:493
  8.0 0.8 reshape.84.cinv
  8.8 0.2 bitcast_select_fusion
  9.0 1.6 %copy.15 = f32[3072,128]{1,0:T(8,128)} copy(f32[3072,128]{0,1:T(8,128)S(1)} %bitcast.31) | data formatting | bytes 3145728 | tf_op jit(solution)/shard_map/transpose | solution.py:491
  10.6 0.0 copy-done
  10.6 82.9 %shard_map.77 = (f32[12,256,128]{2,1,0:T(8,128)}, f32[12,256,128]{2,1,0:T(8,128)}) custom-call(f32[6,512,1536]{2,1,0:T(8,128)} %bitcast.29, f32[12,256,128]{2,1,0:T(8,128)} %bitcast.30, f32[16,3072]{1,0:T(8,128)} %copy-done, s32[1,1280]{1,0:T(1,128)} %get-tuple-element.15.inner0, s32[1,1280]{1,0:T(1,128)} %get-tuple-element.14.inner1, ...), custom_call_target="tpu_custom_call" | custom-call | tf_op jit(solution)/shard_map/pallas_call | solution.py:501
  93.4 0.0 copy-start.1
  93.5 2.8 %copy.26 = f32[2,1536,128]{2,1,0:T(8,128)} copy(f32[2,1536,128]{2,1,0:T(8,128)} %bitcast.34) | data formatting | bytes 3145728
  96.2 0.0 copy-done.1
  96.2 1.1 %copy.27 = f32[2,1536,128]{2,1,0:T(8,128)} copy(f32[2,1536,128]{2,1,0:T(8,128)S(1)} %bitcast.33) | data formatting | bytes 3145728
  (12 shorter events, 0.2 us)
Async XLA Ops:
  6.8 3.7 %copy-start = (f32[16,3072]{1,0:T(8,128)}, f32[16,3072]{1,0:T(8,128)S(1)}, u32[]{:S(2)}) copy-start(f32[16,3072]{1,0:T(8,128)S(1)} %pad_add_fusion.modes) | copy-start | bytes 589828
  93.4 2.8 %copy-start.1 = (f32[12,256,128]{2,1,0:T(8,128)S(1)}, f32[12,256,128]{2,1,0:T(8,128)}, u32[]{:S(2)}) copy-start(f32[12,256,128]{2,1,0:T(8,128)} %get-tuple-element.5) | copy-start | bytes 4718596

commit v2 on v1

--- a/solution.py
+++ b/solution.py
@@ -32,11 +32,11 @@
 
 
 def kernel(
-    ops_hbm, modes_field, modes, inner0, inner1, outer, cinv, rhs, crhs,
+    ops_hbm, modes_in, members, cinv, rhs_hbm, crhs,
     mult, proj,
-    ops_hi, ops_lo, ops_buf, perm0, perm1, share, lift_cat, image_cat, cat,
-    field, jumped, image, past, pool, coarse, near,
-    ops_sem, halo_send, halo_recv, near_send, near_recv, ag_send, ag_recv, fwd_send, fwd_recv,
+    ops_hi, ops_lo, ops_buf, perm0, perm1, share, lift_cat, image_cat, cat, cat2,
+    field, jumped, image, past, pool, coarse, near, near_cat, modes, spread, outer, columns,
+    ops_sem, rhs_sem, halo_send, halo_recv, near_send, near_recv, ag_send, ag_recv, fwd_send, fwd_recv,
     *, clusters,
 ):
     c = lax.axis_index("clus")
@@ -55,49 +55,6 @@
 
     def load(chunk, buf):
         return pltpu.make_async_copy(ops_hbm.at[chunk], ops_buf.at[buf], ops_sem.at[buf])
-
-    load(0, 0).start()
-    load(1, 1).start()
-
-    near[...] = jnp.zeros_like(near)
-    barrier = pltpu.get_barrier_semaphore()
-
-    @pl.loop(1, clusters)
-    def _(k):
-        pl.semaphore_signal(barrier, inc=1, device_id=((c + k) % clusters, t), device_id_type=MESH)
-
-    pl.semaphore_signal(barrier, inc=1, device_id=(c, other), device_id_type=MESH)
-
-    @pl.when(has_up)
-    def _():
-        pl.semaphore_signal(barrier, inc=1, device_id=(up, other), device_id_type=MESH)
-
-    @pl.when(has_down)
-    def _():
-        pl.semaphore_signal(barrier, inc=1, device_id=(down, other), device_id_type=MESH)
-
-    @pl.when(c == 0)
-    def _():
-        for r in range(ROUNDS):
-            pool[r, 256:448, :] = jnp.zeros((192, LANES), F32)
-            pool[r, 640:704, :] = jnp.zeros((64, LANES), F32)
-
-    @pl.when(c == clusters - 1)
-    def _():
-        for r in range(ROUNDS):
-            pool[r, 448:640, :] = jnp.zeros((192, LANES), F32)
-            pool[r, 704:768, :] = jnp.zeros((64, LANES), F32)
-
-    coarse[0, t, c] = crhs[...]
-    near[slot] = cinv[...]
-
-    @pl.when(has_up & has_down)
-    def _():
-        pl.semaphore_wait(barrier, clusters + 2)
-
-    @pl.when(jnp.logical_not(has_up & has_down))
-    def _():
-        pl.semaphore_wait(barrier, clusters + 1)
 
     def halo_copies(source, r):
         top, low = source.at[0], source.at[per]
@@ -228,10 +185,8 @@
         fwd_copy(r, t).wait_send()
         fwd_copy(r, other).wait_recv()
         gathered = coarse[r].reshape(2 * clusters * 16, LANES)
-        weights = jnp.dot(
-            near[...].reshape(LANES, 2 * clusters * 16), gathered,
-            precision=lax.Precision.HIGHEST, preferred_element_type=F32,
-        )
+        out = mm(near_cat[...], split(gathered))
+        weights = fold(out[:LANES]) + out[LANES:, :LANES]
         high = weights.astype(BF16)
         low = (weights - high.astype(F32)).astype(BF16)
         wide = jnp.concatenate(
@@ -240,25 +195,100 @@
         )
         return wide, jnp.sum(gathered.reshape(2 * clusters, 16, LANES), axis=0)
 
+    load(0, 0).start()
+    load(1, 1).start()
+
+    near[...] = jnp.zeros_like(near)
+    barrier = pltpu.get_barrier_semaphore()
+
+    @pl.loop(1, clusters)
+    def _(k):
+        pl.semaphore_signal(barrier, inc=1, device_id=((c + k) % clusters, t), device_id_type=MESH)
+
+    pl.semaphore_signal(barrier, inc=1, device_id=(c, other), device_id_type=MESH)
+
+    @pl.when(has_up)
+    def _():
+        pl.semaphore_signal(barrier, inc=1, device_id=(up, other), device_id_type=MESH)
+
+    @pl.when(has_down)
+    def _():
+        pl.semaphore_signal(barrier, inc=1, device_id=(down, other), device_id_type=MESH)
+
+    rhs_copy = pltpu.make_async_copy(rhs_hbm, past, rhs_sem)
+    rhs_copy.start()
+
+    @pl.when(c == 0)
+    def _():
+        for r in range(ROUNDS):
+            pool[r, 256:448, :] = jnp.zeros((192, LANES), F32)
+            pool[r, 640:704, :] = jnp.zeros((64, LANES), F32)
+
+    @pl.when(c == clusters - 1)
+    def _():
+        for r in range(ROUNDS):
+            pool[r, 448:640, :] = jnp.zeros((192, LANES), F32)
+            pool[r, 704:768, :] = jnp.zeros((64, LANES), F32)
+
+    modes[...] = jnp.zeros_like(modes)
+    for k in range(modes_in.shape[0]):
+        modes[2 * k : 2 * k + 1, :rows] = modes_in[k, 0:1, :]
+        modes[2 * k + 1 : 2 * k + 2, rows:] = modes_in[k, 1:2, :]
+    spread[...] = jnp.zeros_like(spread)
+    spread[pl.ds(pl.multiple_of(slot * 16, 16), 16), :] = modes[...]
+    modes_field = image
+    for n in (0, per):
+        modes_field[n] = jnp.transpose(spread[:, n * TILE : (n + 1) * TILE])
+
+    coarse[0, t, c] = jnp.zeros((16, LANES), F32)
+    for k in range(crhs.shape[0]):
+        coarse[0, t, c, 2 * k : 2 * k + 2, :] = crhs[k]
+    near[slot] = cinv[...]
+
+    @pl.loop(0, inner // TILE)
+    def _(n):
+        at = lax.broadcasted_iota(jnp.int32, (TILE, inner), 0) + n * TILE
+        perm0[n] = (at == members[1, 1:2, ESUB:] - ESUB).astype(F32).astype(BF16)
+        perm1[n] = (at == members[0, 1:2, ESUB:] - (rows + ESUB)).astype(F32).astype(BF16)
+
+    names = jnp.concatenate([members[0, :, :ESUB], members[1, :, :ESUB]], axis=1)
+    offset = names - 2 * rows
+    block = lax.shift_right_arithmetic(offset, 9)
+    within = offset & (2 * ESUB - 1)
+    cluster = lax.shift_right_arithmetic(block, 1)
+    own = (block & 1) == t
+    sibling = jnp.where(within < 128, within, within - 256)
+    lower = jnp.where(own, jnp.where(within < 256, within + 128, within), within + 256)
+    upper = jnp.where(own, jnp.where(within < 384, within + 192, within + 128), within + 256)
+    place = jnp.where(cluster == 0, lower, jnp.where(cluster == 1, sibling, upper))
+    named = names < 2 * rows + 12 * ESUB
+    place = jnp.where(named, place, -1).astype(F32)
+    size = jnp.sum(named.astype(F32), axis=0, keepdims=True)
+    row = lax.broadcasted_iota(jnp.int32, place.shape, 0)
+    outer[...] = jnp.zeros_like(outer)
+    outer[0:4, :] = jnp.where(row == 0, 1.0 / size, place)
+    columns[...] = jnp.transpose(outer[...])
+    at = lax.broadcasted_iota(jnp.int32, (2 * ESUB, POOL), 1).astype(F32)
+    total = jnp.zeros((2 * ESUB, POOL), F32)
+    for n in range(1, 4):
+        total = total + (at == columns[:, n : n + 1]).astype(F32)
+    share[...] = total.astype(BF16)
+
+    @pl.when(has_up & has_down)
+    def _():
+        pl.semaphore_wait(barrier, clusters + 2)
+
+    @pl.when(jnp.logical_not(has_up & has_down))
+    def _():
+        pl.semaphore_wait(barrier, clusters + 1)
+
     start_all(halo_copies(modes_field, 0))
     start_all(near_groups())
     ag_start(0)
 
-    @pl.loop(0, inner // TILE)
-    def _(n):
-        at = lax.broadcasted_iota(jnp.int32, (TILE, inner), 0) + n * TILE
-        perm0[n] = (at == inner1[...]).astype(F32).astype(BF16)
-        perm1[n] = (at == inner0[...]).astype(F32).astype(BF16)
-
-    columns = jnp.transpose(outer[...])
-    at = lax.broadcasted_iota(jnp.int32, (2 * ESUB, POOL), 1).astype(F32)
-    total = jnp.zeros((2 * ESUB, POOL), F32)
-    for n in range(3):
-        total = total + (at == columns[:, n : n + 1]).astype(F32)
-    share[...] = total.astype(BF16)
-
-    def portion():
-        return jnp.transpose(outer[...])[:, 3:4]
+    for n in range(tiles):
+        if n % per:
+            modes_field[n] = jnp.transpose(spread[:, n * TILE : (n + 1) * TILE])
 
     @pl.loop(0, 2 * half)
     def _(chunk):
@@ -278,28 +308,26 @@
             load(chunk + 2, buf).start()
 
     def tile_rows(n):
-        return pl.ds(pl.multiple_of(n * TILE, TILE), TILE)
-
-    def make_cat(source):
-        @pl.loop(0, tiles)
-        def _(n):
-            cat[tile_rows(n), :] = split(source[n])
-
-    def jump(source, r, groups, target):
-        @pl.loop(0, inner // TILE)
-        def _(n):
+        return pl.ds(n * TILE, TILE)
+
+    def jump(source, r, groups, target, target_cat):
+        def emit(n, value):
+            target[n] = value
+            target_cat[n * TILE : (n + 1) * TILE, :] = split(value)
+
+        for n in range(inner // TILE):
             picked = fold(mm(perm0[n], cat[rows + ESUB : 2 * rows, :]))
-            target[1 + n] = 0.5 * (source[1 + n] - picked)
+            emit(1 + n, 0.5 * (source[1 + n] - picked))
             back = fold(mm(perm1[n], cat[ESUB:rows, :]))
-            target[per + 1 + n] = 0.5 * (source[per + 1 + n] - back)
+            emit(per + 1 + n, 0.5 * (source[per + 1 + n] - back))
 
         wait_all(groups)
         picked = fold(mm(share[...], split(pool[r])))
-        scale = portion()
-        target[0] = source[0] - (source[0] + picked[:ESUB]) * scale[:ESUB]
-        target[per] = source[per] - (source[per] + picked[ESUB:]) * scale[ESUB:]
-
-    def big_tile(n, emit):
+        scale = columns[:, 0:1]
+        emit(0, source[0] - (source[0] + picked[:ESUB]) * scale[:ESUB])
+        emit(per, source[per] - (source[per] + picked[ESUB:]) * scale[ESUB:])
+
+    def big_tile(n, emit, cat):
         at_rows = pl.ds(pl.multiple_of((n // half) * rows, TILE), rows)
         out = fold(mm(ops_hi[n], cat[at_rows, :])) + mm(ops_lo[n], cat[at_rows, :LANES])
         emit(n, out)
@@ -315,7 +343,7 @@
         value = modes[...]
         high = value.astype(BF16)
         low = (value - high.astype(F32)).astype(BF16)
-        out = mm(jnp.concatenate([high, low], axis=0), cat[...])
+        out = mm(jnp.concatenate([high, low], axis=0), cat2[...])
         return fold(out[:16]) + out[16:, :LANES]
 
     def put(r, terms, sums):
@@ -327,54 +355,52 @@
     def row_sum(value):
         return jnp.sum(value, axis=0, keepdims=True)
 
-    make_cat(modes_field)
-    jump(modes_field, 0, halo_copies(modes_field, 0), field)
-
-    @pl.loop(0, tiles)
-    def _(n):
-        value = split(field[n])
-        lift_cat[tile_rows(n), :] = value
-        cat[tile_rows(n), :] = value
+    for n in range(tiles):
+        cat[n * TILE : (n + 1) * TILE, :] = split(modes_field[n])
+    jump(modes_field, 0, halo_copies(modes_field, 0), field, lift_cat)
 
     ag_forward(0)
 
     @pl.loop(0, 2 * half)
     def _(n):
-        big_tile(n, store_image_cat)
+        big_tile(n, store_image_cat, lift_cat)
 
     wait_all(near_groups())
+    whole = near[...].reshape(LANES, 2 * clusters * 16)
+    whole_high = whole.astype(BF16)
+    near_cat[:LANES, :] = whole_high
+    near_cat[LANES:, :] = (whole - whole_high.astype(F32)).astype(BF16)
     wide, _ = ag_finish(0)
 
     def start_tile(n):
         mult[n] = fold(mm(lift_cat[tile_rows(n), :], wide))
-        value = rhs[n] - fold(mm(image_cat[tile_rows(n), :], wide))
+        value = past[n] - fold(mm(image_cat[tile_rows(n), :], wide))
         field[n] = value
         cat[tile_rows(n), :] = split(value)
 
+    rhs_copy.wait()
     start_tile(0)
     start_tile(per)
     groups = halo_copies(field, 1)
     start_all(groups)
 
-    @pl.loop(1, per)
-    def _(n):
+    for n in range(1, per):
         start_tile(n)
         start_tile(per + n)
 
-    jump(field, 1, groups, jumped)
-    make_cat(jumped)
+    jump(field, 1, groups, jumped, cat2)
     put(1, restrict(), [])
     ag_start(1)
 
     @pl.loop(0, half)
     def _(n):
-        big_tile(n, store_image)
+        big_tile(n, store_image, cat2)
 
     ag_forward(1)
 
     @pl.loop(half, 2 * half)
     def _(n):
-        big_tile(n, store_image)
+        big_tile(n, store_image, cat2)
 
     wide, _ = ag_finish(1)
 
@@ -390,21 +416,21 @@
     carry = first_tile(per, first_tile(0, (zero, zero)))
     groups = halo_copies(field, 2)
     start_all(groups)
-    carry = lax.fori_loop(1, per, lambda n, now: first_tile(per + n, first_tile(n, now)), carry)
-    jump(field, 2, groups, jumped)
-    make_cat(jumped)
+    for n in range(1, per):
+        carry = first_tile(per + n, first_tile(n, carry))
+    jump(field, 2, groups, jumped, cat2)
     put(2, restrict(), carry)
     ag_start(2)
 
     @pl.loop(0, half)
     def _(n):
-        big_tile(n, store_image)
+        big_tile(n, store_image, cat2)
 
     ag_forward(2)
 
     @pl.loop(half, 2 * half)
     def _(n):
-        big_tile(n, store_image)
+        big_tile(n, store_image, cat2)
 
     wide, sums = ag_finish(2)
     curvature, norm = sums[12:13], sums[13:14]
@@ -431,9 +457,9 @@
     carry = second_tile(per, second_tile(0, (zero, zero, zero)))
     groups = halo_copies(image, 3)
     start_all(groups)
-    carry = lax.fori_loop(1, per, lambda n, now: second_tile(per + n, second_tile(n, now)), carry)
-    jump(image, 3, groups, field)
-    make_cat(field)
+    for n in range(1, per):
+        carry = second_tile(per + n, second_tile(n, carry))
+    jump(image, 3, groups, field, cat2)
     put(3, restrict(), carry)
     ag_start(3)
     ag_forward(3)
@@ -442,8 +468,7 @@
     beta = norm_next / norm
     step_last = norm_next / (fresh + beta * (crossed + beta * curvature))
 
-    @pl.loop(0, tiles)
-    def _(n):
+    for n in range(tiles):
         moved = field[n] - fold(mm(lift_cat[tile_rows(n), :], wide))
         old = proj[n]
         mult[n] = mult[n] + step_last * (old + beta * jumped[n])
@@ -456,52 +481,22 @@
     tiles = subs * rows // TILE
     local_rows = subs * rows
     export = subs * ESUB
-    pad_index = local_rows + 6 * export
     inner = rows - ESUB
-    c = lax.axis_index("clus")
-    t = lax.axis_index("sub")
-    slot = (c % 4) * 2 + t
-
-    inner0 = (members[0, 1, ESUB:] - rows - ESUB)[None, :]
-    inner1 = (members[1, 1, ESUB:] - ESUB)[None, :]
-
-    names = jnp.transpose(members[:, :, :ESUB], (1, 0, 2)).reshape(-1, export)
-    offset = names - local_rows
-    block = offset // export
-    within = offset % export
-    cluster = block // 2
-    own = (block % 2) == t
-    sibling = jnp.where(within < 128, within, within - 256)
-    lower = jnp.where(own, jnp.where(within < 256, within + 128, within), within + 256)
-    upper = jnp.where(own, jnp.where(within < 384, within + 192, within + 128), within + 256)
-    at = jnp.where(cluster == 0, lower, jnp.where(cluster == 1, sibling, upper))
-    at = jnp.where(names < pad_index, at, -1).astype(F32)
-    size = jnp.sum((names < pad_index).astype(F32), axis=0, keepdims=True)
-    outer = jnp.concatenate([at[1:4], 1.0 / size, jnp.zeros((4, export), F32)], axis=0)
 
     count = subs * modes_count
-    modes = jnp.concatenate(
-        [
-            jnp.pad(rigid_modes[0], ((0, 16 - modes_count), (0, rows))),
-        ],
-        axis=0,
-    ) + jnp.pad(rigid_modes[1], ((modes_count, 16 - count), (rows, 0)))
-    lane = lax.broadcasted_iota(jnp.int32, (8, 1, 1), 0)
-    spread = jnp.where(lane == slot, modes[None], 0.0).reshape(LANES, local_rows)
-    modes_field = jnp.transpose(spread).reshape(tiles, TILE, lanes)
-
-    cinv = coarse_inverse.reshape(count, clusters, 2, count).transpose(0, 2, 1, 3)
+    cinv = coarse_inverse.reshape(subs, modes_count, clusters, 2, subs, modes_count)
+    cinv = cinv.transpose(1, 0, 3, 2, 5, 4).reshape(count, 2, clusters, count)
     cinv = jnp.pad(cinv, ((0, 16 - count), (0, 0), (0, 0), (0, 16 - count)))
     cinv = cinv.reshape(16, 2 * clusters * 16)
-    crhs = jnp.pad(coarse_rhs.reshape(count, lanes), ((0, 16 - count), (0, 0)))
 
     big = local_rows // BIG
     vmem = pl.BlockSpec(memory_space=pltpu.VMEM)
+    hbm = pl.BlockSpec(memory_space=pl.ANY)
     shape = jax.ShapeDtypeStruct((tiles, TILE, lanes), F32)
     mult, proj = pl.pallas_call(
         functools.partial(kernel, clusters=clusters),
         out_shape=(shape, shape),
-        in_specs=[pl.BlockSpec(memory_space=pl.ANY)] + [vmem] * 8,
+        in_specs=[hbm, vmem, vmem, vmem, hbm, vmem],
         out_specs=(vmem, vmem),
         scratch_shapes=[
             pltpu.VMEM((big, BIG, rows), BF16),
@@ -513,6 +508,7 @@
             pltpu.VMEM((local_rows, 2 * lanes), BF16),
             pltpu.VMEM((local_rows, 2 * lanes), BF16),
             pltpu.VMEM((local_rows, 2 * lanes), BF16),
+            pltpu.VMEM((local_rows, 2 * lanes), BF16),
             pltpu.VMEM((tiles, TILE, lanes), F32),
             pltpu.VMEM((tiles, TILE, lanes), F32),
             pltpu.VMEM((tiles, TILE, lanes), F32),
@@ -520,7 +516,13 @@
             pltpu.VMEM((ROUNDS, POOL, lanes), F32),
             pltpu.VMEM((ROUNDS, 2, clusters, 16, lanes), F32),
             pltpu.VMEM((8, 16, 2 * clusters * 16), F32),
+            pltpu.VMEM((2 * LANES, 2 * clusters * 16), BF16),
+            pltpu.VMEM((16, local_rows), F32),
+            pltpu.VMEM((LANES, local_rows), F32),
+            pltpu.VMEM((8, export), F32),
+            pltpu.VMEM((export, 8), F32),
             pltpu.SemaphoreType.DMA((2,)),
+            pltpu.SemaphoreType.DMA,
             pltpu.SemaphoreType.DMA((ROUNDS, 8)),
             pltpu.SemaphoreType.DMA((ROUNDS, 8)),
             pltpu.SemaphoreType.DMA((5,)),
@@ -534,8 +536,8 @@
             collective_id=0, has_side_effects=True, vmem_limit_bytes=60 * 2**20
         ),
     )(
-        dual_ops.reshape(big, BIG, rows), modes_field, modes, inner0, inner1, outer, cinv,
-        dual_rhs.reshape(tiles, TILE, lanes), crhs,
+        dual_ops.reshape(big, BIG, rows), jnp.transpose(rigid_modes, (1, 0, 2)), members, cinv,
+        dual_rhs.reshape(tiles, TILE, lanes), jnp.transpose(coarse_rhs, (1, 0, 2)),
     )
     return mult.reshape(subs, rows, lanes), proj.reshape(subs, rows, lanes)
 

time: 97.9 us -> 85.6 us (0.87)
  Pallas kernels: 82.9 us -> 78 us
  other arithmetic: 3.75 us -> 0 us
  local copies, waits for them, and re-layouts: 10 us -> 6.66 us
    pallas_call x1, Pallas kernels: 82.9 us -> 78 us  [on_device(): pl.pallas_call(functools.partial(kernel, clusters=clusters), out_shape=(s...]
    sub x2 -> x0, other arithmetic: 2.05 us -> none  [the longest x1 1.35 us: on_device(): inner1 = (members[1, 1, ESUB:] - ESUB)[None, :]]
    transpose x1, local copies, waits for them, and re-layouts: 1.61 us -> 0.41 us  [on_device(): cinv = cinv.transpose(1, 0, 3, 2, 5, 4).reshape(count, 2, clusters, count)]
    slice x1 -> x0, local copies, waits for them, and re-layouts: 1.02 us -> none  [on_device(): rigid_modes[0]]
    unnamed x9 -> x5, local copies, waits for them, and re-layouts: 4.64 us -> 4.14 us
where the time goes in v2:
time: 85.6 us; the launch traced here: 85.3 us
  Pallas kernels  78 us (91%)
  local copies, waits for them, and re-layouts  6.66 us (8%)
    pallas_call x1, Pallas kernels, on_device(): pl.pallas_call(functools.partial(kernel, clusters=clusters), out_shape=(s...  78 us
    unnamed x5, local copies, waits for them, and re-layouts  4.14 us

profile of v2, /device:TPU:0, one launch (start us, length us, event | category | flops | bytes accessed | tf_op | source)
XLA Modules:
  0.0 85.3 jit_solution(17838293653734364062)
XLA Ops:
  0.6 1.3 %reshape.26 = f32[2,6,16,2,2,6]{5,4,3,2,1,0:T(2,128)S(1)} reshape(f32[12,384]{1,0:T(8,128)} %param.9) | data formatting | bytes 36864 | tf_op jit(solution)/shard_map/reshape | solution.py:487
  2.0 0.4 copy.9
  2.4 0.2 copy.11
  2.6 0.8 reshape.28.cinv
  3.4 78.0 %shard_map.77 = (f32[12,256,128]{2,1,0:T(8,128)}, f32[12,256,128]{2,1,0:T(8,128)}) custom-call(f32[6,512,1536]{2,1,0:T(8,128)} %bitcast.10, f32[6,2,1536]{2,1,0:T(2,128)} %bitcast.16, s32[2,4,1536]{2,1,0:T(4,128)} %members.1, f32[16,512]{1,0:T(8,128)} %reshape.28.cinv, f32[12,256,128]{2,1,0:T(8,128)} %bitcast.11, f32[6,2,128]{2,1,0:T(2,128)} %bitcast.17), custom_call_target="tpu_custom_call" | custom-call | tf_op jit(solution)/shard_map/pallas_call | solution.py:496
  81.4 0.0 copy-start
  81.4 2.8 %copy.14 = f32[2,1536,128]{2,1,0:T(8,128)} copy(f32[2,1536,128]{2,1,0:T(8,128)} %bitcast.13) | data formatting | bytes 3145728
  84.2 0.0 copy-done
  84.2 1.1 %copy.15 = f32[2,1536,128]{2,1,0:T(8,128)} copy(f32[2,1536,128]{2,1,0:T(8,128)S(1)} %bitcast.12) | data formatting | bytes 3145728
  (1 shorter events, 0.0 us)
Async XLA Ops:
  81.4 2.8 %copy-start = (f32[12,256,128]{2,1,0:T(8,128)S(1)}, f32[12,256,128]{2,1,0:T(8,128)}, u32[]{:S(2)}) copy-start(f32[12,256,128]{2,1,0:T(8,128)} %get-tuple-element.5) | copy-start | bytes 4718596
